TPU v7x, 32 devices: a whole 2x2x4 slice. The times are simulated.
32 devices in a mesh: dp: 4 (over z), seq: 2 (over y), mp: 4 (over x, core).
Axes of the slice: x: 2, y: 2, z: 4, core: 2. Of those that a mesh axis runs over, the one named last changes fastest.
Arguments:
- hidden_in: bfloat16 [4, 1024, 768], P('dp', 'seq', 'mp'), may hold values from -6 to 6
- cotangent: bfloat16 [4, 1024, 768], P('dp', 'seq', 'mp'), may hold values from -6 to 6
- attention_gain: float32 [768], replicated, may hold values from 0.1 to 1.9
- feedforward_gain: float32 [768], replicated, may hold values from 0.1 to 1.9
- qkv_weight: bfloat16 [768, 3, 768], P(None, None, 'mp'), may hold values from -0.21875 to 0.21875
- attention_out: bfloat16 [768, 768], P('mp'), may hold values from -0.75 to 0.75
- geglu_in: bfloat16 [768, 2, 1152], P(None, None, 'mp'), may hold values from -0.21875 to 0.21875
- geglu_out: bfloat16 [1152, 768], P('mp'), may hold values from -0.1875 to 0.1875
Outputs:
- layer_out: float32 [4, 1024, 768], P('dp', 'seq', 'mp')
- grad_input: float32 [4, 1024, 768], P('dp', 'seq', 'mp')
- grad_qkv: float32 [768, 3, 768], P(None, None, 'mp')
- grad_attention_out: float32 [768, 768], P('mp')
- grad_geglu_in: float32 [768, 2, 1152], P(None, None, 'mp')
- grad_geglu_out: float32 [1152, 768], P('mp')
- grad_attention_gain: float32 [768], P('mp')
- grad_feedforward_gain: float32 [768], P('mp')
All inputs are finite; a program needn't handle non-finite values.
Results may differ from a plain program's by a relative error of at most 0.018.
Values may be sent and summed in bfloat16 or wider, within the bound.
No kernel may reach another device: no remote copies, remote signals or barrier semaphores. Data moves between devices by JAX's collectives and lax.ppermute only.
A program may use at most 64 MiB of HBM per device.

v0:
```python
import math
import jax
import jax.numpy as jnp
from jax import lax
from jax.sharding import PartitionSpec as P

HEAD = 64
HALF = 64


def with_halo(block, sides, width):
    for axis, dim in sides:
        count = lax.axis_size(axis)
        forward = [(i, i + 1) for i in range(count - 1)]
        backward = [(target, source) for source, target in forward]
        low = lax.ppermute(
            lax.slice_in_dim(block, block.shape[dim] - width, None, axis=dim), axis, forward
        )
        high = lax.ppermute(lax.slice_in_dim(block, 0, width, axis=dim), axis, backward)
        block = jnp.concatenate([low, block, high], axis=dim)
    return block


def normalize(rows):
    center = rows - jnp.mean(rows, axis=-1, keepdims=True)
    inverse = lax.rsqrt(jnp.mean(center * center, axis=-1, keepdims=True) + 1e-05)
    return (center * inverse, inverse)


def frequencies(positions):
    inverse_freq = jnp.exp(
        jnp.arange(HEAD // 2).astype(jnp.float32) * (-2.0 * math.log(10000.0) / HEAD)
    )
    angles = positions[:, None] * inverse_freq[None, :]
    angles = jnp.concatenate([angles, angles], axis=-1)
    return (jnp.cos(angles), jnp.sin(angles))


def rotate(tensor, cosine, sine):
    halfway = HEAD // 2
    turned = jnp.concatenate([-tensor[..., halfway:], tensor[..., :halfway]], axis=-1)
    return tensor * cosine[:, None, :] + turned * sine[:, None, :]


def gelu_exact(value):
    return 0.5 * value * (1.0 + lax.erf(value * 0.7071067811865476))


def gelu_slope(value):
    return (
        0.5 * (1.0 + lax.erf(value * 0.7071067811865476))
        + value * jnp.exp(-0.5 * value * value) * 0.3989422804014327
    )


def windows(wide, tile):
    count = (wide.shape[1] - tile) // tile
    shape = (wide.shape[0], count, tile) + wide.shape[2:]
    lower = wide[:, : count * tile].reshape(shape)
    upper = wide[:, tile:].reshape(shape)
    return jnp.concatenate([lower, upper], axis=2)


def unwindow(grads, tile):
    rest = grads.shape[3:]
    shape = (grads.shape[0], grads.shape[1] * tile) + rest
    lower = grads[:, :, :tile].reshape(shape)
    upper = grads[:, :, tile:].reshape(shape)
    others = ((0, 0),) * len(rest)
    return jnp.pad(lower, ((0, 0), (0, tile)) + others) + jnp.pad(
        upper, ((0, 0), (tile, 0)) + others
    )


def band_mask(base, count, tile, total_length):
    query_off = jnp.arange(tile, dtype=jnp.int32)
    key_off = jnp.arange(2 * tile, dtype=jnp.int32) - HALF
    near = jnp.abs(query_off[:, None] - key_off[None, :]) <= HALF
    key_pos = (
        base
        - HALF
        + jnp.arange(count, dtype=jnp.int32)[:, None] * tile
        + jnp.arange(2 * tile, dtype=jnp.int32)[None, :]
    )
    inside = (key_pos >= 0) & (key_pos < total_length)
    return near[None] & inside[:, None, :]


def attend(queries, keys_wide, values_wide, allowed):
    batch, length, heads, size = queries.shape
    tile = 2 * HALF
    count = length // tile
    query_tiles = queries.reshape(batch, count, tile, heads, size)
    key_tiles = windows(keys_wide, tile)
    value_tiles = windows(values_wide, tile)
    scores = jnp.einsum(
        "snqhd,snkhd->snhqk", query_tiles, key_tiles, preferred_element_type=jnp.float32
    ) * HEAD ** (-0.5)
    scores = jnp.where(allowed[None, :, None], scores, -1e30)
    top = jnp.max(scores, axis=-1, keepdims=True)
    log_total = top + jnp.log(jnp.sum(jnp.exp(scores - top), axis=-1, keepdims=True))
    weights = jnp.exp(scores - log_total).astype(jnp.bfloat16)
    mixed = jnp.einsum(
        "snhqk,snkhd->snqhd", weights, value_tiles, preferred_element_type=jnp.float32
    ).astype(jnp.bfloat16)
    return (mixed.reshape(batch, length, heads, size), log_total)


def attend_back(queries, keys_wide, values_wide, allowed, log_total, mixed, grad_mixed):
    batch, length, heads, size = queries.shape
    tile = 2 * HALF
    count = length // tile
    query_tiles = queries.reshape(batch, count, tile, heads, size)
    key_tiles = windows(keys_wide, tile)
    value_tiles = windows(values_wide, tile)
    grad_tiles = grad_mixed.reshape(batch, count, tile, heads, size)
    again = jnp.einsum(
        "snqhd,snkhd->snhqk", query_tiles, key_tiles, preferred_element_type=jnp.float32
    ) * HEAD ** (-0.5)
    again = jnp.where(allowed[None, :, None], again, -1e30)
    probs = jnp.exp(again - log_total)
    delta = jnp.sum(grad_mixed.astype(jnp.float32) * mixed.astype(jnp.float32), axis=-1)
    delta = jnp.transpose(delta.reshape(batch, count, tile, heads), (0, 1, 3, 2))
    grad_value_tiles = jnp.einsum(
        "snhqk,snqhd->snkhd",
        probs.astype(jnp.bfloat16),
        grad_tiles,
        preferred_element_type=jnp.float32,
    )
    grad_probs = jnp.einsum(
        "snqhd,snkhd->snhqk", grad_tiles, value_tiles, preferred_element_type=jnp.float32
    )
    grad_scores = (probs * (grad_probs - delta[..., None]) * HEAD ** (-0.5)).astype(jnp.bfloat16)
    grad_queries = jnp.einsum(
        "snhqk,snkhd->snqhd", grad_scores, key_tiles, preferred_element_type=jnp.float32
    )
    grad_key_tiles = jnp.einsum(
        "snhqk,snqhd->snkhd", grad_scores, query_tiles, preferred_element_type=jnp.float32
    )
    return (
        grad_queries.reshape(batch, length, heads, size),
        unwindow(grad_key_tiles, tile),
        unwindow(grad_value_tiles, tile),
    )


def edge_rims(grad_packed, length):
    return jnp.concatenate([grad_packed[:, :HALF], grad_packed[:, HALF + length :]], axis=1)


def fold_rims(grad_packed, returned, length):
    lower_add = jnp.pad(returned[:, :HALF], ((0, 0), (0, length - HALF), (0, 0)))
    upper_add = jnp.pad(returned[:, 3 * HALF :], ((0, 0), (length - HALF, 0), (0, 0)))
    return grad_packed[:, HALF : HALF + length] + lower_add + upper_add


def body(
    hidden_in,
    cotangent,
    attention_gain,
    feedforward_gain,
    qkv_weight,
    attention_out,
    geglu_in,
    geglu_out,
):
    batch, length, share = hidden_in.shape
    width = share * lax.axis_size("mp")
    offset = lax.axis_index("mp") * share
    columns = qkv_weight.shape[2]
    heads = columns // HEAD
    span = length + 2 * HALF
    inputs_full, upstream_full = (
        lax.all_gather(hidden_in, "mp", axis=2, tiled=True),
        lax.all_gather(cotangent, "mp", axis=2, tiled=True),
    )
    normed_one, inverse_one = normalize(inputs_full.astype(jnp.float32))
    fed_one = (normed_one * attention_gain).astype(jnp.bfloat16)
    projected = jnp.einsum("std,dch->stch", fed_one, qkv_weight, preferred_element_type=jnp.float32)
    block_index = lax.axis_index("seq")
    total_length = length * lax.axis_size("seq")
    query_pos = block_index * length + jnp.arange(length, dtype=jnp.int32)
    cosine, sine = frequencies(query_pos.astype(jnp.float32))
    queries = rotate(projected[:, :, 0].reshape(batch, length, heads, HEAD), cosine, sine).astype(
        jnp.bfloat16
    )
    keys_own = rotate(projected[:, :, 1].reshape(batch, length, heads, HEAD), cosine, sine).astype(
        jnp.bfloat16
    )
    values_own = projected[:, :, 2].astype(jnp.bfloat16)
    packed = jnp.concatenate([keys_own.reshape(batch, length, columns), values_own], axis=2)
    widened = with_halo(packed, (("seq", 1),), HALF)
    keys_wide = widened[:, :, :columns].reshape(batch, span, heads, HEAD)
    values_wide = widened[:, :, columns:].reshape(batch, span, heads, HEAD)
    allowed = band_mask(block_index * length, length // (2 * HALF), 2 * HALF, total_length)
    mixed, log_total = attend(queries, keys_wide, values_wide, allowed)
    joined = mixed.reshape(batch, length, columns)
    attn_terms = jnp.einsum(
        "sqh,hd->sqd", joined, attention_out, preferred_element_type=jnp.float32
    )
    middle = hidden_in.astype(jnp.float32) + lax.psum_scatter(
        attn_terms, "mp", scatter_dimension=2, tiled=True
    )
    middle_full = lax.all_gather(middle, "mp", axis=2, tiled=True)
    normed_two, inverse_two = normalize(middle_full)
    fed_two = (normed_two * feedforward_gain).astype(jnp.bfloat16)
    lifted = jnp.einsum("std,dcf->stcf", fed_two, geglu_in, preferred_element_type=jnp.float32)
    linear = lifted[:, :, 0]
    gating = lifted[:, :, 1]
    activated = gelu_exact(linear)
    product = (activated * gating).astype(jnp.bfloat16)
    mlp_terms = jnp.einsum("stf,fd->std", product, geglu_out, preferred_element_type=jnp.float32)
    layer_out = middle + lax.psum_scatter(
        mlp_terms.astype(jnp.bfloat16), "mp", scatter_dimension=2, tiled=True
    ).astype(jnp.float32)
    grad_geglu_out = jnp.einsum(
        "stf,std->fd", product, upstream_full, preferred_element_type=jnp.float32
    )
    grad_product = jnp.einsum(
        "std,fd->stf", upstream_full, geglu_out, preferred_element_type=jnp.float32
    )
    grad_linear = grad_product * gating * gelu_slope(linear)
    grad_gating = grad_product * activated
    grad_lifted = jnp.stack([grad_linear, grad_gating], axis=2).astype(jnp.bfloat16)
    grad_geglu_in = jnp.einsum(
        "std,stcf->dcf", fed_two, grad_lifted, preferred_element_type=jnp.float32
    )
    fed_terms = jnp.einsum(
        "stcf,dcf->std", grad_lifted, geglu_in, preferred_element_type=jnp.float32
    )
    grad_fed_two = lax.psum_scatter(fed_terms, "mp", scatter_dimension=2, tiled=True)
    normed_two_own = lax.dynamic_slice_in_dim(normed_two, offset, share, 2)
    gain_two_own = lax.dynamic_slice_in_dim(feedforward_gain, offset, share, 0)
    grad_ff_gain = jnp.sum(grad_fed_two * normed_two_own, axis=(0, 1))
    dhat_two = grad_fed_two * gain_two_own
    first_two, second_two = lax.psum(
        (
            jnp.sum(dhat_two, axis=-1, keepdims=True),
            jnp.sum(dhat_two * normed_two_own, axis=-1, keepdims=True),
        ),
        "mp",
    )
    grad_middle = cotangent.astype(jnp.float32) + inverse_two * (
        dhat_two - first_two / width - normed_two_own * (second_two / width)
    )
    grad_middle_full = lax.all_gather(grad_middle.astype(jnp.bfloat16), "mp", axis=2, tiled=True)
    grad_attention_out = jnp.einsum(
        "sqh,sqd->hd", joined, grad_middle_full, preferred_element_type=jnp.float32
    )
    grad_mixed = jnp.einsum(
        "sqd,hd->sqh", grad_middle_full, attention_out, preferred_element_type=jnp.float32
    ).astype(jnp.bfloat16)
    grad_mixed = grad_mixed.reshape(batch, length, heads, HEAD)
    grad_queries, grad_keys_wide, grad_values_wide = attend_back(
        queries, keys_wide, values_wide, allowed, log_total, mixed, grad_mixed
    )
    grad_packed = jnp.concatenate(
        [
            grad_keys_wide.reshape(batch, span, columns),
            grad_values_wide.reshape(batch, span, columns),
        ],
        axis=2,
    )
    returned = with_halo(
        edge_rims(grad_packed, length).astype(jnp.bfloat16), (("seq", 1),), HALF
    ).astype(jnp.float32)
    grad_own = fold_rims(grad_packed, returned, length)
    grad_keys = rotate(grad_own[:, :, :columns].reshape(batch, length, heads, HEAD), cosine, -sine)
    grad_queries = rotate(grad_queries, cosine, -sine)
    grad_values = grad_own[:, :, columns:].reshape(batch, length, heads, HEAD)
    grad_projected = (
        jnp.stack([grad_queries, grad_keys, grad_values], axis=2)
        .reshape(batch, length, 3, columns)
        .astype(jnp.bfloat16)
    )
    grad_qkv = jnp.einsum(
        "std,stch->dch", fed_one, grad_projected, preferred_element_type=jnp.float32
    )
    one_terms = jnp.einsum(
        "stch,dch->std", grad_projected, qkv_weight, preferred_element_type=jnp.float32
    )
    grad_fed_one = lax.psum_scatter(
        one_terms.astype(jnp.bfloat16), "mp", scatter_dimension=2, tiled=True
    ).astype(jnp.float32)
    normed_one_own = lax.dynamic_slice_in_dim(normed_one, offset, share, 2)
    gain_one_own = lax.dynamic_slice_in_dim(attention_gain, offset, share, 0)
    grad_attn_gain = jnp.sum(grad_fed_one * normed_one_own, axis=(0, 1))
    dhat_one = grad_fed_one * gain_one_own
    first_one, second_one = lax.psum(
        (
            jnp.sum(dhat_one, axis=-1, keepdims=True),
            jnp.sum(dhat_one * normed_one_own, axis=-1, keepdims=True),
        ),
        "mp",
    )
    grad_input = grad_middle + inverse_one * (
        dhat_one - first_one / width - normed_one_own * (second_one / width)
    )
    local_grads = (
        grad_qkv,
        grad_attention_out,
        grad_geglu_in,
        grad_geglu_out,
        grad_attn_gain,
        grad_ff_gain,
    )
    summed = lax.psum(
        (
            local_grads[0],
            local_grads[1],
            local_grads[2],
            local_grads[3],
            local_grads[4],
            local_grads[5],
        ),
        ("dp", "seq"),
    )
    return (layer_out, grad_input, summed[0], summed[1], summed[2], summed[3], summed[4], summed[5])


def solution(mesh):
    in_specs = (
        P("dp", "seq", "mp"),
        P("dp", "seq", "mp"),
        P(),
        P(),
        P(None, None, "mp"),
        P("mp", None),
        P(None, None, "mp"),
        P("mp", None),
    )
    out_specs = (
        P("dp", "seq", "mp"),
        P("dp", "seq", "mp"),
        P(None, None, "mp"),
        P("mp", None),
        P(None, None, "mp"),
        P("mp", None),
        P("mp"),
        P("mp"),
    )
    return jax.shard_map(body, mesh=mesh, in_specs=in_specs, out_specs=out_specs, check_vma=False)
```

profile of v0, /device:TPU:0, one launch (start us, length us, event | category | flops | bytes accessed | tf_op | source)
XLA Modules:
  0.0 433.2 jit_solution(13001490404904794870)
XLA Ops:
  7.3 10.4 %all_gather.12 = bf16[1,512,768]{1,2,0:T(8,128)(2,1)S(1)} all-gather(bf16[1,512,192]{1,2,0:T(8,128)(2,1)} %param.8), channel_id=1, replica_groups=mesh['dp'=4,'seq'=2,'mp'=4] {'mp'}, dimensions={2}, use_global_device_ids=true | all-gather | bytes 983040 | tf_op jit(solution)/shard_map/all_gather | solution.py:174
  21.0 1.1 fusion.46
  22.8 3.4 collective-permute-start
  26.2 1.3 collective-permute-start.1
  27.8 1.7 fusion.81
  30.4 1.0 concatenate.132
  31.4 1.1 fusion.43
  33.0 1.2 pad_maximum_fusion.2
  37.7 2.7 copy.56
  42.3 43.4 %all-reduce.16.cloned.1.call-done = f32[1,512,768]{1,0,2:T(1,128)} async-done(((f32[1,512,768]{1,0,2:T(1,128)}), f32[1,512,768]{1,0,2:T(1,128)}) %all-reduce.16.cloned.1.call-update) | async-done | bytes 1572880
  85.7 2.1 dynamic-slice_add_fusion
  87.9 8.6 %all_gather.14 = bf16[1,512,768]{1,2,0:T(8,128)(2,1)} all-gather(bf16[1,512,192]{1,2,0:T(8,128)(2,1)S(1)} %copy-done.12), channel_id=1, replica_groups=mesh['dp'=4,'seq'=2,'mp'=4] {'mp'}, dimensions={2}, use_global_device_ids=true | all-gather | bytes 983040 | tf_op jit(solution)/shard_map/all_gather | solution.py:175
  96.5 11.2 %all-gather.2.cloned.1.call-done = f32[1,512,768]{1,0,2:T(1,128)} async-done(((f32[1,512,192]{1,0,2:T(1,128)}), f32[1,512,768]{1,0,2:T(1,128)}) %all-gather.2.cloned.1.call-update) | async-done | bytes 1572880 | tf_op jit(solution)/shard_map/all_gather | solution.py:204
  107.7 2.4 reduce_sum.111
  110.4 1.1 copy-done.4
  115.8 2.0 convolution_bitcast_fusion
  117.8 4.8 %copy.60 = f32[1,512,768]{1,0,2:T(1,128)} copy(f32[1,512,768]{2,1,0:T(8,128)} %convolution_bitcast_fusion) | data formatting | bytes 3145728 | tf_op jit(solution)/shard_map/stcf,dcf->std/dot_general | solution.py:228
  123.6 2.9 fusion.6
  126.6 4.8 %copy.86 = bf16[1,512,768]{1,0,2:T(2,128)(2,1)} copy(bf16[1,512,768]{2,1,0:T(8,128)(2,1)} %fusion.6) | data formatting | bytes 1572864
  131.3 2.5 copy.151
  133.9 31.7 %all-reduce.18.cloned.1.call-done = f32[1,512,768]{1,0,2:T(1,128)} async-done(((f32[1,512,768]{1,0,2:T(1,128)}), f32[1,512,768]{1,0,2:T(1,128)}) %all-reduce.18.cloned.1.call-update) | async-done | bytes 1572880
  165.6 1.3 constant_dynamic-slice_fusion
  167.8 6.0 %all-reduce.11 = (f32[1,512,1]{1,2,0:T(1,128)S(1)}, f32[1,512,1]{1,2,0:T(1,128)S(1)}) all-reduce(f32[1,512,1]{1,2,0:T(1,128)S(1)} %bitcast.303, f32[1,512,1]{1,2,0:T(1,128)S(1)} %bitcast.304), channel_id=1, replica_groups=mesh['dp'=4,'seq'=2,'mp'=4] {'mp'}, use_global_device_ids=true, to_apply=%region_12.13 | all-reduce | flops 1024 | bytes 8192 | tf_op jit(solution)/shard_map/psum | solution.py:236
  173.8 1.2 fusion.98
  175.0 8.3 %all_gather.15 = bf16[1,512,768]{1,2,0:T(8,128)(2,1)S(1)} all-gather(bf16[1,512,192]{1,2,0:T(8,128)(2,1)S(1)} %fusion.98), channel_id=1, replica_groups=mesh['dp'=4,'seq'=2,'mp'=4] {'mp'}, dimensions={2}, use_global_device_ids=true | all-gather | bytes 983040 | tf_op jit(solution)/shard_map/all_gather | solution.py:246
  185.3 1.6 fusion.47
  187.0 2.1 convolution_bitcast_fusion.3
  193.4 3.4 collective-permute-start.2
  196.8 1.3 collective-permute-start.3
  199.4 4.1 collective-permute-done.3
  206.1 1.7 fusion.5
  207.9 4.8 %copy.88 = bf16[1,512,768]{1,0,2:T(2,128)(2,1)} copy(bf16[1,512,768]{2,1,0:T(8,128)(2,1)} %fusion.5) | data formatting | bytes 1572864
  212.6 2.5 copy.150
  215.2 2.9 fusion.16
  218.1 1.9 fusion.48
  220.1 1.2 fusion.13
  221.4 2.0 fusion.76
  223.5 1.4 fusion
  224.9 1.4 fusion.44
  227.1 10.6 %reduce-scatter.9.cloned.1.call-done = bf16[192,512]{1,0:T(8,128)(2,1)} async-done(((bf16[768,512]{1,0:T(8,128)(2,1)}), bf16[192,512]{1,0:T(8,128)(2,1)}) %reduce-scatter.9.cloned.1.call-update) | async-done | bytes 196624
  237.7 1.1 reshape_bitcast_fusion
  238.8 1.2 fusion.37
  240.0 22.6 %all-reduce.8 = (f32[192]{0:T(256)}, f32[192]{0:T(256)}) all-reduce(f32[192]{0:T(256)S(1)} %get-tuple-element.34, f32[192]{0:T(256)S(1)} %get-tuple-element.32), channel_id=1, replica_groups=mesh['dp'=4,'seq'=2,'mp'=4] {'dp','seq'}, use_global_device_ids=true, to_apply=%region_24.25 | all-reduce | flops 384 | bytes 3072 | tf_op jit(solution)/shard_map/psum | solution.py:307
  262.6 6.0 %all-reduce.10 = (f32[1,512,1]{1,2,0:T(1,128)S(1)}, f32[1,512,1]{1,2,0:T(1,128)S(1)}) all-reduce(f32[1,512,1]{1,2,0:T(1,128)S(1)} %bitcast.301, f32[1,512,1]{1,2,0:T(1,128)S(1)} %bitcast.302), channel_id=1, replica_groups=mesh['dp'=4,'seq'=2,'mp'=4] {'mp'}, use_global_device_ids=true, to_apply=%region_18.19 | all-reduce | flops 1024 | bytes 8192 | tf_op jit(solution)/shard_map/psum | solution.py:289
  268.7 2.0 fusion.35
  270.7 149.2 %all-reduce.20.cloned.1.call-done = (f32[768,3,192]{0,2,1:T(8,128)}, f32[192,768]{1,0:T(8,128)}, f32[768,2,288]{0,2,1:T(8,128)}, f32[288,768]{1,0:T(8,128)}) async-done(((f32[768,3,192]{0,2,1:T(8,128)}, f32[192,768]{1,0:T(8,128)}, f32[768,2,288]{0,2,1:T(8,128)}, f32[288,768]{1,0:T(8,128)}), (f32[768,3,192]{0,2,1:T(8,128)}, f32[192,768]{1,0:T(8,128)}, f32[768,2,288]{0,2,1:T(8,128)}, ...) | async-done | bytes 5013520 | tf_op jit(solution)/shard_map/psum | solution.py:307
  419.9 2.9 copy.158
  423.7 1.2 copy.160
  (203 shorter events, 30.0 us)
Async XLA Ops:
  7.2 10.9 %copy-start = (bf16[768,3,192]{0,2,1:T(8,128)(2,1)S(1)}, bf16[768,3,192]{0,2,1:T(8,128)(2,1)}, u32[]{:S(2)}) copy-start(bf16[768,3,192]{0,2,1:T(8,128)(2,1)} %param.12) | copy-start | bytes 2654212
  7.2 10.9 %copy-start.47 = (f32[768]{0:T(1024)S(1)}, f32[768]{0:T(1024)}, u32[]{:S(2)}) copy-start(f32[768]{0:T(1024)} %param.10) | copy-start | bytes 9220
  7.2 78.5 %all-reduce.16.cloned.1.call-start = ((), (), s32[]{:S(2)}) async-start(), calls=%async_computation.5 | async-start | bytes 3145728
  18.8 1.0 copy-start.17
  20.9 1.9 copy-start.18
  22.8 9.8 %collective-permute-start = (bf16[1,64,384]{1,2,0:T(8,128)(2,1)}, bf16[1,64,384]{1,2,0:T(8,128)(2,1)S(1)}, u32[]{:S(2)}, u32[]{:S(2)}) collective-permute-start(bf16[1,64,384]{1,2,0:T(8,128)(2,1)} %get-tuple-element.71), channel_id=1, source_target_pairs={{0,4},{1,5},{2,6},{3,7},{8,12},{9,13},{10,14},{11,15},{16,20},{17,... | collective-permute-start | bytes 147464 | tf_op jit(solution)/shard_map/ppermute | solution.py:16
  26.2 6.8 %collective-permute-start.1 = (bf16[1,64,384]{1,2,0:T(8,128)(2,1)S(1)}, bf16[1,64,384]{1,2,0:T(8,128)(2,1)}, u32[]{:S(2)}, u32[]{:S(2)}) collective-permute-start(bf16[1,64,384]{1,2,0:T(8,128)(2,1)S(1)} %get-tuple-element.72), channel_id=1, source_target_pairs={{4,0},{5,1},{6,2},{7,3},{12,8},{13,9},{14,10},{15,11},{20,16},{21,... | collective-permute-start | bytes 147464 | tf_op jit(solution)/shard_map/ppermute | solution.py:19
  32.6 1.9 copy-start.24
  35.1 1.2 copy-start.1
  35.8 1.5 copy-start.20
  40.4 45.3 %copy-start.35 = (bf16[1,512,192]{1,2,0:T(8,128)(2,1)S(1)}, bf16[1,512,192]{1,2,0:T(8,128)(2,1)}, u32[]{:S(2)}) copy-start(bf16[1,512,192]{1,2,0:T(8,128)(2,1)} %param.8) | copy-start | bytes 589828
  40.4 47.5 %copy-start.12 = (bf16[1,512,192]{1,2,0:T(8,128)(2,1)S(1)}, bf16[1,512,192]{1,2,0:T(8,128)(2,1)}, u32[]{:S(2)}) copy-start(bf16[1,512,192]{1,2,0:T(8,128)(2,1)} %param.9) | copy-start | bytes 589828
  40.5 67.3 %all-gather.2.cloned.1.call-start = ((), (), s32[]{:S(2)}) async-start(), calls=%async_computation.2 | async-start | bytes 1966080 | tf_op jit(solution)/shard_map/all_gather | solution.py:204
  87.9 77.7 %all-reduce.18.cloned.1.call-start = ((), (), s32[]{:S(2)}) async-start(), calls=%async_computation.6 | async-start | bytes 3145728
  107.7 2.4 copy-start.3
  110.1 1.4 copy-start.4
  111.5 1.2 copy-start.22
  111.5 1.2 copy-start.46
  112.7 1.1 copy-start.9
  112.7 1.2 copy-start.48
  114.0 1.0 copy-start.10
  122.6 102.3 %reduce-scatter.7.cloned.1.call-start = ((), (), s32[]{:S(2)}) async-start(), calls=%async_computation.3 | async-start | bytes 983040
  133.8 40.0 %copy-start.13 = (bf16[1,512,192]{1,2,0:T(8,128)(2,1)S(1)}, bf16[1,512,192]{1,2,0:T(8,128)(2,1)}, u32[]{:S(2)}) copy-start(bf16[1,512,192]{1,2,0:T(8,128)(2,1)} %param.9) | copy-start | bytes 589828
  133.9 103.9 %reduce-scatter.9.cloned.1.call-start = ((), (), s32[]{:S(2)}) async-start(), calls=%async_computation.4 | async-start | bytes 983040
  173.8 10.4 %copy-start.21 = (bf16[192,768]{1,0:T(8,128)(2,1)S(1)}, bf16[192,768]{1,0:T(8,128)(2,1)}, u32[]{:S(2)}) copy-start(bf16[192,768]{1,0:T(8,128)(2,1)} %param.13) | copy-start | bytes 884740
  185.3 3.8 copy-start.26
  187.0 2.2 copy-start.2
  187.0 2.2 copy-start.32
  187.0 2.2 copy-start.34
  189.2 0.9 copy-start.28
  189.2 1.0 copy-start.30
  189.2 1.4 copy-start.25
  193.4 5.9 %collective-permute-start.2 = (bf16[1,64,384]{1,2,0:T(8,128)(2,1)S(1)}, bf16[1,64,384]{1,2,0:T(8,128)(2,1)S(1)}, u32[]{:S(2)}, u32[]{:S(2)}) collective-permute-start(bf16[1,64,384]{1,2,0:T(8,128)(2,1)S(1)} %get-tuple-element.53), channel_id=1, source_target_pairs={{0,4},{1,5},{2,6},{3,7},{8,12},{9,13},{10,14},{11,15},{16,20},{17,... | collective-permute-start | bytes 147464 | tf_op jit(solution)/shard_map/ppermute | solution.py:16
  196.8 6.7 %collective-permute-start.3 = (bf16[1,64,384]{1,2,0:T(8,128)(2,1)S(1)}, bf16[1,64,384]{1,2,0:T(8,128)(2,1)S(1)}, u32[]{:S(2)}, u32[]{:S(2)}) collective-permute-start(bf16[1,64,384]{1,2,0:T(8,128)(2,1)S(1)} %get-tuple-element.54), channel_id=1, source_target_pairs={{4,0},{5,1},{6,2},{7,3},{12,8},{13,9},{14,10},{15,11},{20,16},{21,... | collective-permute-start | bytes 147464 | tf_op jit(solution)/shard_map/ppermute | solution.py:19
  204.1 0.9 copy-start.41
  204.1 1.0 copy-start.19
  215.1 204.8 %all-reduce.20.cloned.1.call-start = ((), (), s32[]{:S(2)}) async-start(), calls=%async_computation.7 | async-start | bytes 10027008 | tf_op jit(solution)/shard_map/psum | solution.py:307
  215.2 2.9 copy-start.43
  215.2 2.9 copy-start.45
  218.1 2.0 copy-start.6
  218.1 2.0 copy-start.16
  220.1 1.3 copy-start.37
  220.1 1.3 copy-start.39
  224.9 43.8 %copy-start.8 = (f32[1,512,192]{1,0,2:T(1,128)S(1)}, f32[1,512,192]{1,0,2:T(1,128)}, u32[]{:S(2)}) copy-start(f32[1,512,192]{1,0,2:T(1,128)} %copy-done.7) | copy-start | bytes 1179652
  224.9 43.8 %copy-start.14 = (bf16[1,512,192]{1,2,0:T(8,128)(2,1)S(1)}, bf16[1,512,192]{1,2,0:T(8,128)(2,1)}, u32[]{:S(2)}) copy-start(bf16[1,512,192]{1,2,0:T(8,128)(2,1)} %param.9) | copy-start | bytes 589828
  419.9 3.0 copy-start.40
  419.9 3.8 copy-start.11
  423.7 1.8 copy-start.23
  (12 other events, 8.8 us)
Sparse Core Ops, SparseCore 0:
  40.6 45.0 all-reduce.15
  88.0 19.6 all-gather.1
  122.7 42.8 all-reduce.17
  168.0 23.2 reduce-scatter.6
  215.3 22.4 reduce-scatter.8
  242.1 177.7 all-reduce.19
where the time goes:
time: 434 us; the launch traced here: 433 us
  waiting for transfers between devices  251 us (58%)
  blocking collectives  61.9 us (14%)
  local copies, waits for them, and re-layouts  47.5 us (11%)
  other arithmetic  25.6 us (6%)
  matrix products  21.8 us (5%)
  between operations  15.6 us (4%)
  starting transfers between devices  9.63 us (2%)
    psum x1, waiting for transfers between devices, body(): lax.psum((local_grads[0], local_grads[1], local_grads[2], local_grads[3],...  149 us
    unnamed x10, waiting for transfers between devices  85.8 us
    unnamed x117, local copies, waits for them, and re-layouts  34.8 us
    psum x1, blocking collectives, body(): lax.psum((local_grads[0], local_grads[1], local_grads[2], local_grads[3],...  22.6 us
    all_gather x1, waiting for transfers between devices, body(): middle_full = lax.all_gather(middle, 'mp', axis=2, tiled=True)  11.2 us
    all_gather x1, blocking collectives, body(): lax.all_gather(hidden_in, 'mp', axis=2, tiled=True)  10.4 us
  transfers between devices with their start and end apart: 10, of which 8 were waited for; matrix products, arithmetic and copies ran while one was open for 13% of the time, Pallas kernels for 0%

commit v1 on v0

--- a/solution.py
+++ b/solution.py
@@ -305,15 +305,18 @@
         grad_ff_gain,
     )
     summed = lax.psum(
-        (
-            local_grads[0],
-            local_grads[1],
-            local_grads[2],
-            local_grads[3],
-            local_grads[4],
-            local_grads[5],
+        lax.psum(
+            (
+                local_grads[0],
+                local_grads[1],
+                local_grads[2],
+                local_grads[3],
+                local_grads[4],
+                local_grads[5],
+            ),
+            "seq",
         ),
-        ("dp", "seq"),
+        "dp",
     )
     return (layer_out, grad_input, summed[0], summed[1], summed[2], summed[3], summed[4], summed[5])
 

time: 434 us -> 582 us (1.34)
  waiting for transfers between devices: 251 us -> 406 us
    psum x0 -> x1, waiting for transfers between devices: none -> 156 us  [body(): lax.psum(lax.psum((local_grads[0], local_grads[1], local_grads[2], local_...]
    psum x1, waiting for transfers between devices: 149 us -> 104 us  [body(): lax.psum((local_grads[0], local_grads[1], local_grads[2], local_grads[3],...]
    unnamed x10 -> x11, waiting for transfers between devices: 85.8 us -> 126 us
    psum x1, blocking collectives: 22.6 us -> 4.93 us  [body(): lax.psum((local_grads[0], local_grads[1], local_grads[2], local_grads[3],...]
    psum x0 -> x1, blocking collectives: none -> 12.9 us  [body(): lax.psum(lax.psum((local_grads[0], local_grads[1], local_grads[2], local_...]
    unnamed x117 -> x109, local copies, waits for them, and re-layouts: 34.8 us -> 33.4 us
  transfers between devices with their start and end apart: 10 -> 11, of which waited for: 8 -> 10; matrix products, arithmetic and copies ran while one was open for 13% -> 6% of each run, Pallas kernels for 0% -> 0%
where the time goes in v1:
time: 582 us; the launch traced here: 580 us
  waiting for transfers between devices  406 us (70%)
  blocking collectives  57.1 us (10%)
  local copies, waits for them, and re-layouts  45.1 us (8%)
  other arithmetic  23.3 us (4%)
  matrix products  22.9 us (4%)
  between operations  15.7 us (3%)
  starting transfers between devices  10.3 us (2%)
    psum x1, waiting for transfers between devices, body(): lax.psum(lax.psum((local_grads[0], local_grads[1], local_grads[2], local_...  156 us
    unnamed x11, waiting for transfers between devices  126 us
    psum x1, waiting for transfers between devices, body(): lax.psum((local_grads[0], local_grads[1], local_grads[2], local_grads[3],...  104 us
    unnamed x109, local copies, waits for them, and re-layouts  33.4 us
    psum x1, blocking collectives, body(): lax.psum(lax.psum((local_grads[0], local_grads[1], local_grads[2], local_...  12.9 us
  transfers between devices with their start and end apart: 11, of which 10 were waited for; matrix products, arithmetic and copies ran while one was open for 6% of the time, Pallas kernels for 0%

profile of v1, /device:TPU:0, one launch (start us, length us, event | category | flops | bytes accessed | tf_op | source)
XLA Modules:
  0.0 580.3 jit_solution(14251380701560206734)
XLA Ops:
  7.3 10.4 %all_gather.12 = bf16[1,512,768]{1,2,0:T(8,128)(2,1)S(1)} all-gather(bf16[1,512,192]{1,2,0:T(8,128)(2,1)} %param.8), channel_id=1, replica_groups=mesh['dp'=4,'seq'=2,'mp'=4] {'mp'}, dimensions={2}, use_global_device_ids=true | all-gather | bytes 983040 | tf_op jit(solution)/shard_map/all_gather | solution.py:174
  22.8 4.1 collective-permute-start
  26.9 1.3 collective-permute-start.1
  30.1 3.8 collective-permute-done.1
  33.9 1.2 pad_maximum_fusion.2
  38.6 2.7 copy.56
  43.2 41.0 %all-reduce.19.cloned.1.call-done = f32[1,512,768]{1,0,2:T(1,128)} async-done(((f32[1,512,768]{1,0,2:T(1,128)}), f32[1,512,768]{1,0,2:T(1,128)}) %all-reduce.19.cloned.1.call-update) | async-done | bytes 1572880
  84.2 2.1 dynamic-slice_add_fusion
  86.5 8.6 %all_gather.14 = bf16[1,512,768]{1,2,0:T(8,128)(2,1)} all-gather(bf16[1,512,192]{1,2,0:T(8,128)(2,1)S(1)} %copy-done.10), channel_id=1, replica_groups=mesh['dp'=4,'seq'=2,'mp'=4] {'mp'}, dimensions={2}, use_global_device_ids=true | all-gather | bytes 983040 | tf_op jit(solution)/shard_map/all_gather | solution.py:175
  95.1 11.2 %all-gather.2.cloned.1.call-done = f32[1,512,768]{1,0,2:T(1,128)} async-done(((f32[1,512,192]{1,0,2:T(1,128)}), f32[1,512,768]{1,0,2:T(1,128)}) %all-gather.2.cloned.1.call-update) | async-done | bytes 1572880 | tf_op jit(solution)/shard_map/all_gather | solution.py:204
  106.3 2.4 reduce_sum.111
  108.9 1.1 copy-done.4
  114.4 2.0 convolution_bitcast_fusion
  116.3 4.8 copy.60
  122.2 2.9 fusion.16
  125.1 1.9 fusion.48
  127.0 37.1 %all-reduce.21.cloned.1.call-done = f32[1,512,768]{1,0,2:T(1,128)} async-done(((f32[1,512,768]{1,0,2:T(1,128)}), f32[1,512,768]{1,0,2:T(1,128)}) %all-reduce.21.cloned.1.call-update) | async-done | bytes 1572880
  164.2 1.3 constant_dynamic-slice_fusion
  166.4 6.0 %all-reduce.9 = (f32[1,512,1]{1,2,0:T(1,128)S(1)}, f32[1,512,1]{1,2,0:T(1,128)S(1)}) all-reduce(f32[1,512,1]{1,2,0:T(1,128)S(1)} %bitcast.303, f32[1,512,1]{1,2,0:T(1,128)S(1)} %bitcast.304), channel_id=1, replica_groups=mesh['dp'=4,'seq'=2,'mp'=4] {'mp'}, use_global_device_ids=true, to_apply=%region_12.13 | all-reduce | flops 1024 | bytes 8192 | tf_op jit(solution)/shard_map/psum | solution.py:236
  172.4 1.2 fusion.98
  173.6 8.3 %all_gather.15 = bf16[1,512,768]{1,2,0:T(8,128)(2,1)S(1)} all-gather(bf16[1,512,192]{1,2,0:T(8,128)(2,1)S(1)} %fusion.98), channel_id=1, replica_groups=mesh['dp'=4,'seq'=2,'mp'=4] {'mp'}, dimensions={2}, use_global_device_ids=true | all-gather | bytes 983040 | tf_op jit(solution)/shard_map/all_gather | solution.py:246
  182.2 1.2 fusion.13
  184.2 1.6 fusion.47
  185.9 2.1 convolution_bitcast_fusion.3
  192.3 3.4 collective-permute-start.2
  195.7 1.3 collective-permute-start.3
  198.3 4.1 collective-permute-done.3
  204.4 2.0 fusion.76
  206.4 2.9 fusion.6
  209.4 4.8 copy.86
  214.2 2.5 copy.151
  216.8 2.8 fusion.5
  219.6 4.8 copy.88
  224.4 2.5 copy.150
  227.0 104.4 %all-reduce.25.cloned.1.call-done = (f32[768,3,192]{0,2,1:T(8,128)}, f32[192,768]{1,0:T(8,128)}, f32[768,2,288]{0,2,1:T(8,128)}, f32[288,768]{1,0:T(8,128)}) async-done(((f32[768,3,192]{0,2,1:T(8,128)}, f32[192,768]{1,0:T(8,128)}, f32[768,2,288]{0,2,1:T(8,128)}, f32[288,768]{1,0:T(8,128)}), (f32[768,3,192]{0,2,1:T(8,128)}, f32[192,768]{1,0:T(8,128)}, f32[768,2,288]{0,2,1:T(8,128)}, ...) | async-done | bytes 5013520 | tf_op jit(solution)/shard_map/psum | solution.py:308
  331.5 1.4 fusion
  332.9 24.2 %reduce-scatter.7.cloned.1.call-done = bf16[192,512]{1,0:T(8,128)(2,1)} async-done(((bf16[768,512]{1,0:T(8,128)(2,1)}), bf16[192,512]{1,0:T(8,128)(2,1)}) %reduce-scatter.7.cloned.1.call-update) | async-done | bytes 196624
  357.1 1.4 fusion.44
  359.2 23.5 %reduce-scatter.9.cloned.1.call-done = bf16[192,512]{1,0:T(8,128)(2,1)} async-done(((bf16[768,512]{1,0:T(8,128)(2,1)}), bf16[192,512]{1,0:T(8,128)(2,1)}) %reduce-scatter.9.cloned.1.call-update) | async-done | bytes 196624
  382.7 1.1 reshape_bitcast_fusion
  383.8 1.2 fusion.37
  385.0 4.9 all-reduce.12
  389.9 12.9 %all-reduce.10 = (f32[192]{0:T(256)}, f32[192]{0:T(256)}) all-reduce(f32[192]{0:T(256)S(1)} %get-tuple-element.48, f32[192]{0:T(256)S(1)} %get-tuple-element.49), channel_id=1, replica_groups=mesh['dp'=4,'seq'=2,'mp'=4] {'dp'}, use_global_device_ids=true, to_apply=%region_29.30 | all-reduce | flops 384 | bytes 3072 | tf_op jit(solution)/shard_map/psum | solution.py:307
  402.8 6.0 %all-reduce.8 = (f32[1,512,1]{1,2,0:T(1,128)S(1)}, f32[1,512,1]{1,2,0:T(1,128)S(1)}) all-reduce(f32[1,512,1]{1,2,0:T(1,128)S(1)} %bitcast.299, f32[1,512,1]{1,2,0:T(1,128)S(1)} %bitcast.300), channel_id=1, replica_groups=mesh['dp'=4,'seq'=2,'mp'=4] {'mp'}, use_global_device_ids=true, to_apply=%region_18.19 | all-reduce | flops 1024 | bytes 8192 | tf_op jit(solution)/shard_map/psum | solution.py:289
  408.9 2.0 fusion.35
  410.9 156.1 %all-reduce.23.cloned.1.call-done = (f32[768,3,192]{0,2,1:T(8,128)}, f32[192,768]{1,0:T(8,128)}, f32[768,2,288]{0,2,1:T(8,128)}, f32[288,768]{1,0:T(8,128)}) async-done(((f32[768,3,192]{0,2,1:T(8,128)}, f32[192,768]{1,0:T(8,128)}, f32[768,2,288]{0,2,1:T(8,128)}, f32[288,768]{1,0:T(8,128)}), (f32[768,3,192]{0,2,1:T(8,128)}, f32[192,768]{1,0:T(8,128)}, f32[768,2,288]{0,2,1:T(8,128)}, ...) | async-done | bytes 5013520 | tf_op jit(solution)/shard_map/psum | solution.py:307
  567.0 2.9 copy.162
  570.8 1.2 copy.164
  (199 shorter events, 29.8 us)
Async XLA Ops:
  7.2 10.9 %copy-start = (bf16[768,3,192]{0,2,1:T(8,128)(2,1)S(1)}, bf16[768,3,192]{0,2,1:T(8,128)(2,1)}, u32[]{:S(2)}) copy-start(bf16[768,3,192]{0,2,1:T(8,128)(2,1)} %param.12) | copy-start | bytes 2654212
  7.2 10.9 %copy-start.43 = (f32[768]{0:T(1024)S(1)}, f32[768]{0:T(1024)}, u32[]{:S(2)}) copy-start(f32[768]{0:T(1024)} %param.10) | copy-start | bytes 9220
  7.2 77.0 %all-reduce.19.cloned.1.call-start = ((), (), s32[]{:S(2)}) async-start(), calls=%async_computation.5 | async-start | bytes 3145728
  18.8 1.0 copy-start.15
  20.9 1.9 copy-start.16
  22.8 7.3 %collective-permute-start = (bf16[1,64,384]{1,2,0:T(8,128)(2,1)}, bf16[1,64,384]{1,2,0:T(8,128)(2,1)}, u32[]{:S(2)}, u32[]{:S(2)}) collective-permute-start(bf16[1,64,384]{1,2,0:T(8,128)(2,1)} %get-tuple-element.77), channel_id=1, source_target_pairs={{0,4},{1,5},{2,6},{3,7},{8,12},{9,13},{10,14},{11,15},{16,20},{17,... | collective-permute-start | bytes 147464 | tf_op jit(solution)/shard_map/ppermute | solution.py:16
  26.9 7.0 %collective-permute-start.1 = (bf16[1,64,384]{1,2,0:T(8,128)(2,1)}, bf16[1,64,384]{1,2,0:T(8,128)(2,1)}, u32[]{:S(2)}, u32[]{:S(2)}) collective-permute-start(bf16[1,64,384]{1,2,0:T(8,128)(2,1)} %get-tuple-element.78), channel_id=1, source_target_pairs={{4,0},{5,1},{6,2},{7,3},{12,8},{13,9},{14,10},{15,11},{20,16},{21,... | collective-permute-start | bytes 147464 | tf_op jit(solution)/shard_map/ppermute | solution.py:19
  30.0 5.4 copy-start.22
  36.0 1.2 copy-start.1
  36.6 1.5 copy-start.18
  41.3 42.9 %copy-start.33 = (bf16[1,512,192]{1,2,0:T(8,128)(2,1)S(1)}, bf16[1,512,192]{1,2,0:T(8,128)(2,1)}, u32[]{:S(2)}) copy-start(bf16[1,512,192]{1,2,0:T(8,128)(2,1)} %param.8) | copy-start | bytes 589828
  41.3 45.1 %copy-start.10 = (bf16[1,512,192]{1,2,0:T(8,128)(2,1)S(1)}, bf16[1,512,192]{1,2,0:T(8,128)(2,1)}, u32[]{:S(2)}) copy-start(bf16[1,512,192]{1,2,0:T(8,128)(2,1)} %param.9) | copy-start | bytes 589828
  41.3 64.9 %all-gather.2.cloned.1.call-start = ((), (), s32[]{:S(2)}) async-start(), calls=%async_computation.2 | async-start | bytes 1966080 | tf_op jit(solution)/shard_map/all_gather | solution.py:204
  86.4 77.8 %all-reduce.21.cloned.1.call-start = ((), (), s32[]{:S(2)}) async-start(), calls=%async_computation.6 | async-start | bytes 3145728
  106.3 2.4 copy-start.3
  108.7 1.4 copy-start.4
  110.1 1.2 copy-start.20
  110.1 1.2 copy-start.42
  111.2 1.1 copy-start.7
  111.3 1.2 copy-start.44
  112.5 1.0 copy-start.8
  121.2 210.2 %all-reduce.25.cloned.1.call-start = ((), (), s32[]{:S(2)}) async-start(), calls=%async_computation.8 | async-start | bytes 10027008 | tf_op jit(solution)/shard_map/psum | solution.py:308
  121.2 3.9 copy-start.39
  121.2 3.9 copy-start.41
  127.0 45.3 %copy-start.11 = (bf16[1,512,192]{1,2,0:T(8,128)(2,1)S(1)}, bf16[1,512,192]{1,2,0:T(8,128)(2,1)}, u32[]{:S(2)}) copy-start(bf16[1,512,192]{1,2,0:T(8,128)(2,1)} %param.9) | copy-start | bytes 589828
  172.3 9.6 %copy-start.19 = (bf16[192,768]{1,0:T(8,128)(2,1)S(1)}, bf16[192,768]{1,0:T(8,128)(2,1)}, u32[]{:S(2)}) copy-start(bf16[192,768]{1,0:T(8,128)(2,1)} %param.13) | copy-start | bytes 884740
  172.3 9.9 %copy-start.14 = (bf16[1,4,128,3,64]{2,1,4,3,0:T(4,128)(2,1)S(1)}, bf16[1,4,128,3,64]{2,1,4,3,0:T(4,128)(2,1)}, u32[]{:S(2)}) copy-start(bf16[1,4,128,3,64]{2,1,4,3,0:T(4,128)(2,1)} %copy-done.13) | copy-start | bytes 589828
  184.2 3.8 copy-start.24
  185.9 2.2 copy-start.2
  185.9 2.2 copy-start.30
  185.9 2.2 copy-start.32
  188.1 0.9 copy-start.26
  188.1 1.0 copy-start.28
  188.1 1.4 copy-start.23
  192.3 5.9 %collective-permute-start.2 = (bf16[1,64,384]{1,2,0:T(8,128)(2,1)S(1)}, bf16[1,64,384]{1,2,0:T(8,128)(2,1)S(1)}, u32[]{:S(2)}, u32[]{:S(2)}) collective-permute-start(bf16[1,64,384]{1,2,0:T(8,128)(2,1)S(1)} %get-tuple-element.59), channel_id=1, source_target_pairs={{0,4},{1,5},{2,6},{3,7},{8,12},{9,13},{10,14},{11,15},{16,20},{17,... | collective-permute-start | bytes 147464 | tf_op jit(solution)/shard_map/ppermute | solution.py:16
  195.7 6.7 %collective-permute-start.3 = (bf16[1,64,384]{1,2,0:T(8,128)(2,1)S(1)}, bf16[1,64,384]{1,2,0:T(8,128)(2,1)S(1)}, u32[]{:S(2)}, u32[]{:S(2)}) collective-permute-start(bf16[1,64,384]{1,2,0:T(8,128)(2,1)S(1)} %get-tuple-element.60), channel_id=1, source_target_pairs={{4,0},{5,1},{6,2},{7,3},{12,8},{13,9},{14,10},{15,11},{20,16},{21,... | collective-permute-start | bytes 147464 | tf_op jit(solution)/shard_map/ppermute | solution.py:19
  203.0 0.9 copy-start.37
  203.0 1.0 copy-start.17
  204.3 2.1 copy-start.34
  204.3 2.1 copy-start.35
  206.4 150.7 %reduce-scatter.7.cloned.1.call-start = ((), (), s32[]{:S(2)}) async-start(), calls=%async_computation.3 | async-start | bytes 983040
  216.7 166.0 %reduce-scatter.9.cloned.1.call-start = ((), (), s32[]{:S(2)}) async-start(), calls=%async_computation.4 | async-start | bytes 983040
  226.9 340.1 %all-reduce.23.cloned.1.call-start = ((), (), s32[]{:S(2)}) async-start(), calls=%async_computation.7 | async-start | bytes 10027008 | tf_op jit(solution)/shard_map/psum | solution.py:307
  332.9 76.0 %copy-start.6 = (f32[1,512,192]{1,0,2:T(1,128)S(1)}, f32[1,512,192]{1,0,2:T(1,128)}, u32[]{:S(2)}) copy-start(f32[1,512,192]{1,0,2:T(1,128)} %copy-done.5) | copy-start | bytes 1179652
  332.9 76.0 %copy-start.12 = (bf16[1,512,192]{1,2,0:T(8,128)(2,1)S(1)}, bf16[1,512,192]{1,2,0:T(8,128)(2,1)}, u32[]{:S(2)}) copy-start(bf16[1,512,192]{1,2,0:T(8,128)(2,1)} %param.9) | copy-start | bytes 589828
  567.0 3.0 copy-start.36
  567.0 3.8 copy-start.9
  570.8 1.8 copy-start.21
  (9 other events, 6.5 us)
Sparse Core Ops, SparseCore 0:
  41.5 42.7 all-reduce.18
  86.5 19.6 all-gather.1
  121.3 42.8 all-reduce.20
  206.5 124.8 all-reduce.24
  333.8 23.2 reduce-scatter.6
  359.4 23.2 reduce-scatter.8
  385.3 181.6 all-reduce.22
